TPU v7x, 32 devices: a whole 2x2x4 slice. The times are simulated.
32 devices in a mesh: row: 4 (over y, x), col: 8 (over z, core).
Axes of the slice: x: 2, y: 2, z: 4, core: 2. Of those that a mesh axis runs over, the one named last changes fastest.
Arguments:
- vectors: bfloat16 [64, 131072], P(None, ('col', 'row')), may hold values from -6 to 6
- blocks: bfloat16 [4, 4096, 128, 128], P('row', 'col'), may hold values from -0.1875 to 0.1875
- block_rows: int32 [4, 4096], P('row', 'col'), may hold values from 0 to 255, as said below
- block_cols: int32 [4, 4096], P('row', 'col'), may hold values from 0 to 127, as said below
- counts: int32 [4, 8], P('row', 'col'), may hold values from 1 to 512, as said below
Outputs:
- result: float32 [64, 131072], P(None, ('row', 'col'))
Inputs may be any that keep to these rules, and one draw needn't show every extreme that they name: Within one owner pair the slots below its count name distinct positions (block_rows, block_cols) of its 256 x 256/2 grid of blocks; later slots hold 0. `block_cols`: see block_rows. `counts`: some owner pair holds exactly 512 blocks, and some other exactly one.
All inputs are finite; a program needn't handle non-finite values.
Results may differ from a plain program's by a relative error of at most 0.0029.
Values may be sent and summed in bfloat16 or wider, within the bound.
No kernel may reach another device: no remote copies, remote signals or barrier semaphores. Data moves between devices by JAX's collectives and lax.ppermute only.
A program may use at most 128 MiB of HBM per device.

v0:
```python
import jax
import jax.numpy as jnp
from jax import lax
from jax.sharding import PartitionSpec as P


def from_root(block, axis, owner):
    block = jnp.where(lax.axis_index(axis) == owner, block, jnp.zeros_like(block))
    return lax.psum(block, axis)


def block_product(vec_panel, blocks, block_rows, block_cols, counts):
    slot_total = blocks.shape[1]
    tile_size = blocks.shape[2]
    vec_width = vec_panel.shape[0]
    row_blocks = 2 * vec_panel.shape[1] // tile_size
    vec_tiles = vec_panel.reshape(vec_width, -1, tile_size)
    picked = jnp.take(vec_tiles, block_cols.reshape(-1), axis=1)
    product = jnp.einsum("ksc,src->ksr", picked, blocks[0], preferred_element_type=jnp.float32)
    live_slots = jnp.arange(slot_total, dtype=jnp.int32) < counts.reshape(())
    owner_map = (block_rows == jnp.arange(row_blocks, dtype=jnp.int32)[:, None]) & live_slots[
        None, :
    ]
    summed = jnp.einsum(
        "is,ksr->kir", owner_map.astype(jnp.float32), product, precision=lax.Precision.HIGHEST
    )
    return summed.reshape(vec_width, row_blocks * tile_size)


def relay_group(group_rows):
    half_width = group_rows.shape[1] // 2
    col_owner = lax.axis_index("col")
    own_half = lax.dynamic_slice_in_dim(group_rows, col_owner % 2 * half_width, half_width, 1)
    return from_root(own_half, "row", col_owner // 2)


def shards(vectors, blocks, block_rows, block_cols, counts):
    vec_panel = lax.all_gather(vectors, "row", axis=1, tiled=True)
    first_part = block_product(vec_panel, blocks, block_rows, block_cols, counts)
    group_rows = lax.psum(first_part, "col").astype(jnp.bfloat16)
    second_panel = relay_group(group_rows)
    second_part = block_product(second_panel, blocks, block_rows, block_cols, counts)
    return lax.psum_scatter(second_part, "col", scatter_dimension=1, tiled=True)


def solution(mesh):
    in_specs = (
        P(None, ("col", "row")),
        P("row", "col", None, None),
        P("row", "col"),
        P("row", "col"),
        P("row", "col"),
    )
    out_specs = P(None, ("row", "col"))
    return jax.shard_map(shards, mesh=mesh, in_specs=in_specs, out_specs=out_specs, check_vma=False)
```

profile of v0, /device:TPU:0, one launch (start us, length us, event | category | flops | bytes accessed | tf_op | source)
XLA Modules:
  0.0 559.0 jit_solution(10236251056222093758)
XLA Ops:
  6.5 0.0 all-gather.2.cloned.1.call-start
  6.5 0.7 all-gather.2.cloned.1.call-update
  7.3 0.0 all-reduce.3.cloned.1.call-start
  8.0 0.7 compare_select_fusion
  8.7 0.7 compare_and_fusion
  9.4 37.7 %all-gather.2.cloned.1.call-done = bf16[64,16384]{1,0:T(8,128)(2,1)} async-done(((bf16[64,4096]{1,0:T(8,128)(2,1)}), bf16[64,16384]{1,0:T(8,128)(2,1)}) %all-gather.2.cloned.1.call-update) | async-done | bytes 2097168 | tf_op jit(solution)/shard_map/all_gather | solution.py:38
  47.1 2.2 copy_bitcast_fusion.3
  49.3 13.5 %gather_fusion = bf16[512,64,128]{2,1,0:T(8,128)(2,1)} fusion(bf16[64,128,128]{2,0,1:T(8,128)(2,1)S(1)} %copy_bitcast_fusion.3, s32[1024]{0:T(1024)S(1)} %pad_clamp_fusion), kind=kCustom, calls=%fused_computation.clone | custom fusion | bytes 16779264 | tf_op jit(solution)/shard_map/jit(_take)/gather | solution.py:18
  62.8 0.0 copy-start
  62.8 20.4 %fusion.8 = f32[64,512,128]{2,0,1:T(8,128)} fusion(bf16[1,512,128,128]{3,2,1,0:T(8,128)(2,1)} %param.8, bf16[512,64,128]{2,1,0:T(8,128)(2,1)} %gather_fusion, pred[512]{0:T(512)(128)(4,1)S(1)} %compare_and_fusion), kind=kOutput, calls=%fused_computation.10 | convolution fusion | flops 1077936128 | bytes 41943552 | tf_op jit(solution)/shard_map/ksc,src->ksr/dot_general | solution.py:19
  83.2 0.0 copy-done
  83.2 27.8 %fusion.22 = f32[64,256,128]{1,2,0:T(8,128)} fusion(f32[64,512,128]{2,0,1:T(8,128)} %fusion.8, s32[512]{0:T(512)S(1)} %bitcast.53, pred[512]{0:T(512)(128)(4,1)S(1)} %iota_compare_fusion.1), kind=kOutput, calls=%fused_computation.23 | convolution fusion | flops 12885164032 | bytes 25168384 | tf_op jit(solution)/shard_map/is,ksr->kir/dot_general | solution.py:24
  111.0 9.2 %copy.10 = f32[64,256,128]{2,1,0:T(8,128)} copy(f32[64,256,128]{1,2,0:T(8,128)} %fusion.22) | data formatting | bytes 16777216 | tf_op jit(solution)/shard_map/is,ksr->kir/transpose | solution.py:24
  120.2 11.3 %copy.31 = f32[8,8,256,128]{3,1,2,0:T(8,128)} copy(f32[8,8,256,128]{3,2,1,0:T(8,128)} %bitcast.50) | data formatting | bytes 16777216
  131.5 170.1 %all-reduce.4 = bf16[64,32768]{1,0:T(8,128)(2,1)} all-reduce(f32[64,32768]{1,0:T(8,128)} %bitcast.51), channel_id=1, replica_groups=mesh['row'=4,'col'=8] {'col'}, use_global_device_ids=true, to_apply=%region_0.0 | all-reduce | flops 2097152 | bytes 12582912 | tf_op jit(solution)/shard_map/psum | solution.py:40
  301.6 3.5 copy_bitcast_fusion.2
  305.1 0.0 all-reduce.3.cloned.1.call-update
  305.1 0.0 reduce-scatter.2.cloned.1.call-start
  305.2 67.0 %all-reduce.3.cloned.1.call-done = bf16[64,128,128]{2,0,1:T(8,128)(2,1)} async-done(((bf16[64,128,128]{2,0,1:T(8,128)(2,1)}), bf16[64,128,128]{2,0,1:T(8,128)(2,1)}) %all-reduce.3.cloned.1.call-update) | async-done | bytes 2097168 | tf_op jit(solution)/shard_map/psum | solution.py:9
  372.2 21.6 %gather_fusion.1 = bf16[512,64,128]{2,1,0:T(8,128)(2,1)} fusion(bf16[64,128,128]{2,0,1:T(8,128)(2,1)} %all-reduce.3.cloned.1.call-done, s32[1024]{0:T(1024)S(1)} %pad_clamp_fusion), kind=kCustom, calls=%fused_computation.1.clone | custom fusion | bytes 16779264 | tf_op jit(solution)/shard_map/jit(_take)/gather | solution.py:18
  393.8 20.5 %fusion.11 = f32[64,512,128]{2,0,1:T(8,128)} fusion(bf16[1,512,128,128]{3,2,1,0:T(8,128)(2,1)} %param.8, bf16[512,64,128]{2,1,0:T(8,128)(2,1)} %gather_fusion.1, pred[512]{0:T(512)(128)(4,1)S(1)} %compare_and_fusion), kind=kOutput, calls=%fused_computation.11 | convolution fusion | flops 1077936128 | bytes 41943552 | tf_op jit(solution)/shard_map/ksc,src->ksr/dot_general | solution.py:19
  414.3 27.8 %fusion.25 = f32[64,256,128]{1,2,0:T(8,128)} fusion(f32[64,512,128]{2,0,1:T(8,128)} %fusion.11, s32[512]{0:T(512)S(1)} %bitcast.54, pred[512]{0:T(512)(128)(4,1)S(1)} %iota_compare_fusion.1), kind=kOutput, calls=%fused_computation.24 | convolution fusion | flops 12885164032 | bytes 25168384 | tf_op jit(solution)/shard_map/is,ksr->kir/dot_general | solution.py:24
  442.0 9.2 %copy.13 = f32[64,256,128]{2,1,0:T(8,128)} copy(f32[64,256,128]{1,2,0:T(8,128)} %fusion.25) | data formatting | bytes 16777216 | tf_op jit(solution)/shard_map/is,ksr->kir/transpose | solution.py:24
  451.2 11.3 %copy.30 = f32[8,8,256,128]{3,1,2,0:T(8,128)} copy(f32[8,8,256,128]{3,2,1,0:T(8,128)} %bitcast.52) | data formatting | bytes 16777216
  462.5 0.0 reduce-scatter.2.cloned.1.call-update
  462.6 89.7 %reduce-scatter.2.cloned.1.call-done = f32[64,4096]{1,0:T(8,128)} async-done(((f32[64,32768]{1,0:T(8,128)}), f32[64,4096]{1,0:T(8,128)}) %reduce-scatter.2.cloned.1.call-update) | async-done | bytes 1048592 | tf_op jit(solution)/shard_map/reduce_scatter | solution.py:43
  (2 shorter events, 0.0 us)
Async XLA Ops:
  6.5 40.6 %all-gather.2.cloned.1.call-start = ((), (), s32[]{:S(2)}) async-start(), calls=%async_computation.1 | async-start | bytes 2621440 | tf_op jit(solution)/shard_map/all_gather | solution.py:38
  7.3 364.9 %all-reduce.3.cloned.1.call-start = ((), (), s32[]{:S(2)}) async-start(), calls=%async_computation.2 | async-start | bytes 4194304 | tf_op jit(solution)/shard_map/psum | solution.py:9
  62.8 20.5 %copy-start = (s32[1,512]{1,0:T(1,128)S(1)}, s32[1,512]{1,0:T(1,128)}, u32[]{:S(2)}) copy-start(s32[1,512]{1,0:T(1,128)} %param.9) | copy-start | bytes 6148
  305.1 247.1 %reduce-scatter.2.cloned.1.call-start = ((), (), s32[]{:S(2)}) async-start(), calls=%async_computation.3 | async-start | bytes 9437184 | tf_op jit(solution)/shard_map/reduce_scatter | solution.py:43
Sparse Core Ops, SparseCore 0:
  9.2 37.8 all-gather.1
  305.3 66.8 all-reduce.2
  462.7 89.5 reduce-scatter.1
where the time goes:
time: 565 us; the launch traced here: 559 us
  waiting for transfers between devices  195 us (35%)
  blocking collectives  170 us (30%)
  matrix products  96.5 us (17%)
  local copies, waits for them, and re-layouts  78.3 us (14%)
  between operations  14 us (2%)
    psum x1, blocking collectives, shards(): group_rows = lax.psum(first_part, 'col').astype(jnp.bfloat16)  170 us
    reduce_scatter x1, waiting for transfers between devices, shards(): return lax.psum_scatter(second_part, 'col', scatter_dimension=1, tiled=True)  89.7 us
    psum x1, waiting for transfers between devices, from_root(): return lax.psum(block, axis)  67 us
    dot_general x2, matrix products, block_product(): jnp.einsum('is,ksr->kir', owner_map.astype(jnp.float32), product, precisi...  55.6 us
    dot_general x2, matrix products, block_product(): jnp.einsum('ksc,src->ksr', picked, blocks[0], preferred_element_type=jnp....  40.9 us
    all_gather x1, waiting for transfers between devices, shards(): vec_panel = lax.all_gather(vectors, 'row', axis=1, tiled=True)  37.7 us
    gather x2, local copies, waits for them, and re-layouts, block_product(): picked = jnp.take(vec_tiles, block_cols.reshape(-1), axis=1)  35.1 us
    unnamed x4, local copies, waits for them, and re-layouts  22.7 us
  transfers between devices with their start and end apart: 3, of which 3 were waited for; matrix products, arithmetic and copies ran while one was open for 0% of the time, Pallas kernels for 0%

commit v1 on v0

--- a/solution.py
+++ b/solution.py
@@ -6,7 +6,7 @@
 
 def from_root(block, axis, owner):
     block = jnp.where(lax.axis_index(axis) == owner, block, jnp.zeros_like(block))
-    return lax.psum(block, axis)
+    return jnp.sum(lax.all_gather(block, axis), axis=0)
 
 
 def block_product(vec_panel, blocks, block_rows, block_cols, counts):

time: 565 us -> 584 us (1.034)
  waiting for transfers between devices: 195 us -> 213 us
  other arithmetic: 4.89 us -> 11.6 us
    all_gather x0 -> x1, waiting for transfers between devices: none -> 85 us  [from_root(): return jnp.sum(lax.all_gather(block, axis), axis=0)]
    psum x1 -> x0, waiting for transfers between devices: 67 us -> none  [from_root(): return lax.psum(block, axis)]
    gather x2, local copies, waits for them, and re-layouts: 35.1 us -> 26.9 us  [block_product(): picked = jnp.take(vec_tiles, block_cols.reshape(-1), axis=1)]
    reduce_sum x0 -> x1, other arithmetic: none -> 6.86 us  [from_root(): return jnp.sum(lax.all_gather(block, axis), axis=0)]
where the time goes in v1:
time: 584 us; the launch traced here: 578 us
  waiting for transfers between devices  213 us (36%)
  blocking collectives  170 us (29%)
  matrix products  96.5 us (17%)
  local copies, waits for them, and re-layouts  72.5 us (12%)
  between operations  14.1 us (2%)
  other arithmetic  11.6 us (2%)
    psum x1, blocking collectives, shards(): group_rows = lax.psum(first_part, 'col').astype(jnp.bfloat16)  170 us
    reduce_scatter x1, waiting for transfers between devices, shards(): return lax.psum_scatter(second_part, 'col', scatter_dimension=1, tiled=True)  89.7 us
    all_gather x1, waiting for transfers between devices, from_root(): return jnp.sum(lax.all_gather(block, axis), axis=0)  85 us
    dot_general x2, matrix products, block_product(): jnp.einsum('is,ksr->kir', owner_map.astype(jnp.float32), product, precisi...  55.6 us
    dot_general x2, matrix products, block_product(): jnp.einsum('ksc,src->ksr', picked, blocks[0], preferred_element_type=jnp....  40.9 us
    all_gather x1, waiting for transfers between devices, shards(): vec_panel = lax.all_gather(vectors, 'row', axis=1, tiled=True)  37.7 us
    gather x2, local copies, waits for them, and re-layouts, block_product(): picked = jnp.take(vec_tiles, block_cols.reshape(-1), axis=1)  26.9 us
    unnamed x4, local copies, waits for them, and re-layouts  22.7 us
  transfers between devices with their start and end apart: 3, of which 3 were waited for; matrix products, arithmetic and copies ran while one was open for 0% of the time, Pallas kernels for 0%

profile of v1, /device:TPU:0, one launch (start us, length us, event | category | flops | bytes accessed | tf_op | source)
XLA Modules:
  0.0 577.9 jit_solution(15148139664071196771)
XLA Ops:
  6.5 0.0 all-gather.4.cloned.1.call-start
  6.5 0.7 all-gather.4.cloned.1.call-update
  7.3 0.0 all-gather.6.cloned.1.call-start
  8.0 0.7 compare_select_fusion
  8.7 0.7 compare_and_fusion
  9.4 37.7 %all-gather.4.cloned.1.call-done = bf16[64,16384]{1,0:T(8,128)(2,1)} async-done(((bf16[64,4096]{1,0:T(8,128)(2,1)}), bf16[64,16384]{1,0:T(8,128)(2,1)}) %all-gather.4.cloned.1.call-update) | async-done | bytes 2097168 | tf_op jit(solution)/shard_map/all_gather | solution.py:38
  47.1 2.2 copy_bitcast_fusion.3
  49.3 13.5 %gather_fusion = bf16[512,64,128]{2,1,0:T(8,128)(2,1)} fusion(bf16[64,128,128]{2,0,1:T(8,128)(2,1)S(1)} %copy_bitcast_fusion.3, s32[1024]{0:T(1024)S(1)} %pad_clamp_fusion), kind=kCustom, calls=%fused_computation.clone | custom fusion | bytes 16779264 | tf_op jit(solution)/shard_map/jit(_take)/gather | solution.py:18
  62.8 0.0 copy-start
  62.8 20.4 %fusion.8 = f32[64,512,128]{2,0,1:T(8,128)} fusion(bf16[1,512,128,128]{3,2,1,0:T(8,128)(2,1)} %param.8, bf16[512,64,128]{2,1,0:T(8,128)(2,1)} %gather_fusion, pred[512]{0:T(512)(128)(4,1)S(1)} %compare_and_fusion), kind=kOutput, calls=%fused_computation.10 | convolution fusion | flops 1077936128 | bytes 41943552 | tf_op jit(solution)/shard_map/ksc,src->ksr/dot_general | solution.py:19
  83.2 0.0 copy-done
  83.2 27.8 %fusion.22 = f32[64,256,128]{1,2,0:T(8,128)} fusion(f32[64,512,128]{2,0,1:T(8,128)} %fusion.8, s32[512]{0:T(512)S(1)} %bitcast.55, pred[512]{0:T(512)(128)(4,1)S(1)} %iota_compare_fusion.1), kind=kOutput, calls=%fused_computation.23 | convolution fusion | flops 12885164032 | bytes 25168384 | tf_op jit(solution)/shard_map/is,ksr->kir/dot_general | solution.py:24
  111.0 9.4 %copy.10 = f32[64,256,128]{2,1,0:T(8,128)} copy(f32[64,256,128]{1,2,0:T(8,128)} %fusion.22) | data formatting | bytes 16777216 | tf_op jit(solution)/shard_map/is,ksr->kir/transpose | solution.py:24
  120.4 11.3 %copy.31 = f32[8,8,256,128]{3,1,2,0:T(8,128)} copy(f32[8,8,256,128]{3,2,1,0:T(8,128)} %bitcast.51) | data formatting | bytes 16777216
  131.7 170.1 %all-reduce.1 = bf16[64,32768]{1,0:T(8,128)(2,1)} all-reduce(f32[64,32768]{1,0:T(8,128)} %bitcast.52), channel_id=1, replica_groups=mesh['row'=4,'col'=8] {'col'}, use_global_device_ids=true, to_apply=%region_0.0 | all-reduce | flops 2097152 | bytes 12582912 | tf_op jit(solution)/shard_map/psum | solution.py:40
  301.8 3.3 fusion.28
  305.1 0.0 all-gather.6.cloned.1.call-update
  305.1 0.0 reduce-scatter.2.cloned.1.call-start
  305.2 85.0 %all-gather.6.cloned.1.call-done = bf16[256,16384]{1,0:T(8,128)(2,1)} async-done(((bf16[64,16384]{1,0:T(8,128)(2,1)}), bf16[256,16384]{1,0:T(8,128)(2,1)}) %all-gather.6.cloned.1.call-update) | async-done | bytes 8388624 | tf_op jit(solution)/shard_map/all_gather | solution.py:9
  390.2 6.9 %reduce_sum.12 = bf16[64,16384]{1,0:T(8,128)(2,1)} reduce(bf16[4,64,16384]{2,1,0:T(8,128)(2,1)} %bitcast.54, bf16[]{:T(256)} %constant.50.clone.1), dimensions={0}, to_apply=%region_1.3 | reduce | flops 3145728 | bytes 10485762 | tf_op jit(solution)/shard_map/reduce_sum | solution.py:9
  397.0 2.2 copy_bitcast_fusion.2
  399.2 13.5 %gather_fusion.1 = bf16[512,64,128]{2,1,0:T(8,128)(2,1)} fusion(bf16[64,128,128]{2,0,1:T(8,128)(2,1)S(1)} %copy_bitcast_fusion.2, s32[1024]{0:T(1024)S(1)} %pad_clamp_fusion), kind=kCustom, calls=%fused_computation.1.clone | custom fusion | bytes 16779264 | tf_op jit(solution)/shard_map/jit(_take)/gather | solution.py:18
  412.7 20.4 %fusion.11 = f32[64,512,128]{2,0,1:T(8,128)} fusion(bf16[1,512,128,128]{3,2,1,0:T(8,128)(2,1)} %param.8, bf16[512,64,128]{2,1,0:T(8,128)(2,1)} %gather_fusion.1, pred[512]{0:T(512)(128)(4,1)S(1)} %compare_and_fusion), kind=kOutput, calls=%fused_computation.11 | convolution fusion | flops 1077936128 | bytes 41943552 | tf_op jit(solution)/shard_map/ksc,src->ksr/dot_general | solution.py:19
  433.1 27.8 %fusion.25 = f32[64,256,128]{1,2,0:T(8,128)} fusion(f32[64,512,128]{2,0,1:T(8,128)} %fusion.11, s32[512]{0:T(512)S(1)} %bitcast.56, pred[512]{0:T(512)(128)(4,1)S(1)} %iota_compare_fusion.1), kind=kOutput, calls=%fused_computation.24 | convolution fusion | flops 12885164032 | bytes 25168384 | tf_op jit(solution)/shard_map/is,ksr->kir/dot_general | solution.py:24
  460.9 9.2 %copy.13 = f32[64,256,128]{2,1,0:T(8,128)} copy(f32[64,256,128]{1,2,0:T(8,128)} %fusion.25) | data formatting | bytes 16777216 | tf_op jit(solution)/shard_map/is,ksr->kir/transpose | solution.py:24
  470.1 11.3 %copy.30 = f32[8,8,256,128]{3,1,2,0:T(8,128)} copy(f32[8,8,256,128]{3,2,1,0:T(8,128)} %bitcast.53) | data formatting | bytes 16777216
  481.4 0.0 reduce-scatter.2.cloned.1.call-update
  481.4 89.7 %reduce-scatter.2.cloned.1.call-done = f32[64,4096]{1,0:T(8,128)} async-done(((f32[64,32768]{1,0:T(8,128)}), f32[64,4096]{1,0:T(8,128)}) %reduce-scatter.2.cloned.1.call-update) | async-done | bytes 1048592 | tf_op jit(solution)/shard_map/reduce_scatter | solution.py:43
  (2 shorter events, 0.0 us)
Async XLA Ops:
  6.5 40.6 %all-gather.4.cloned.1.call-start = ((), (), s32[]{:S(2)}) async-start(), calls=%async_computation.1 | async-start | bytes 2621440 | tf_op jit(solution)/shard_map/all_gather | solution.py:38
  7.3 382.9 %all-gather.6.cloned.1.call-start = ((), (), s32[]{:S(2)}) async-start(), calls=%async_computation.3 | async-start | bytes 10485760 | tf_op jit(solution)/shard_map/all_gather | solution.py:9
  62.8 20.5 %copy-start = (s32[1,512]{1,0:T(1,128)S(1)}, s32[1,512]{1,0:T(1,128)}, u32[]{:S(2)}) copy-start(s32[1,512]{1,0:T(1,128)} %param.9) | copy-start | bytes 6148
  305.1 266.0 %reduce-scatter.2.cloned.1.call-start = ((), (), s32[]{:S(2)}) async-start(), calls=%async_computation.2 | async-start | bytes 9437184 | tf_op jit(solution)/shard_map/reduce_scatter | solution.py:43
Sparse Core Ops, SparseCore 0:
  9.2 37.8 all-gather.3
  305.3 84.8 all-gather.5
  481.6 89.4 reduce-scatter.1
